TPU v7x, 32 devices: a whole 2x2x4 slice. The times are simulated.
32 devices in a mesh: row: 4 (over y, x), col: 8 (over z, core).
Axes of the slice: x: 2, y: 2, z: 4, core: 2. Of those that a mesh axis runs over, the one named last changes fastest.
Arguments:
- xblocks: bfloat16 [56, 8, 128, 128], P('row', 'col'), may hold values from -2 to 2
- xcols: int32 [56, 8], P('row', 'col'), may hold values from 0 to 6, as said below
- outcols: int32 [56, 16], P('row', 'col'), may hold values from 0 to 6, as said below
Outputs:
- square_blocks: bfloat16 [56, 16, 128, 128], P('row', 'col')
Inputs may be any that keep to these rules, and one draw needn't show every extreme that they name: xcols[m, t] is a block column within column tile t; over all block rows, the entries of one column tile take at most 3 distinct values. `outcols`: each entry names a block column of its column tile at which at least one block product of the window for that block row lands; entries of one row and tile may repeat.
All inputs are finite; a program needn't handle non-finite values.
Results may differ from a plain program's by a relative error of at most 0.001.
Values may be sent and summed in bfloat16 or wider, within the bound.
A program may use at most 64 MiB of HBM per device.

v0:
```python
import jax
import jax.numpy as jnp
from jax import lax
from jax.sharding import PartitionSpec as P

STEPS = 4


def passed_along(value, axis, steps):
    count = lax.axis_size(axis)
    pairs = [(source, (source + steps) % count) for source in range(count)]
    return lax.ppermute(value, axis, pairs)


def broadcast(value, axis, source):
    kept = jnp.where(lax.axis_index(axis) == source, value, 0).astype(value.dtype)
    return lax.psum(kept, axis)


def add_products(total, a_blocks, a_cols, b_blocks, b_cols, targets, offset):
    index = offset + a_cols
    chosen = jnp.take(b_blocks, index, axis=0)
    landing = jnp.take(b_cols, index, axis=0)
    product = jnp.einsum("mab,mbc->mac", a_blocks, chosen, preferred_element_type=jnp.float32)
    weight = (landing[:, None] == targets).astype(jnp.float32)
    return total + weight[:, :, None, None] * product[:, None]


def on_device(xblocks, xcols, outcols):
    row_count = lax.axis_size("row")
    col_count = lax.axis_size("col")
    per_panel = col_count // row_count
    block_rows = xblocks.shape[0]
    tile_cols = block_rows // per_panel
    block_size = xblocks.shape[2]
    kept = outcols.shape[1]
    row_here = lax.axis_index("row")
    own_blocks = xblocks[:, 0]
    own_cols = xcols[:, 0]
    total = jnp.zeros((block_rows, kept, block_size, block_size), jnp.float32)
    moving = (own_blocks, own_cols)
    for step_no in range(STEPS):
        panel = (row_here + step_no) % row_count
        if step_no > 0:
            moving = passed_along((moving[0], moving[1]), "row", -1)
        for half_no in range(per_panel):
            tile_blocks, tile_cols_ids = (
                broadcast(own_blocks, "col", per_panel * panel + half_no),
                broadcast(own_cols, "col", per_panel * panel + half_no),
            )
            total = add_products(
                total,
                tile_blocks,
                tile_cols_ids,
                moving[0],
                moving[1],
                outcols,
                half_no * tile_cols,
            )
    return total.astype(jnp.bfloat16)


def solution(mesh):
    in_specs = (P("row", "col", None, None), P("row", "col"), P("row", "col"))
    out_specs = P("row", "col", None, None)
    return jax.shard_map(
        on_device, mesh=mesh, in_specs=in_specs, out_specs=out_specs, check_vma=False
    )
```

profile of v0, /device:TPU:0, one launch (start us, length us, event | category | flops | bytes accessed | tf_op | source)
XLA Modules:
  0.0 120.9 jit_solution(17391470564263204695)
XLA Ops:
  6.5 0.0 all-reduce.4.cloned.1.call-start
  6.5 3.9 %collective-permute-start.1 = (bf16[14,128,128]{2,1,0:T(8,128)(2,1)}, bf16[14,128,128]{2,1,0:T(8,128)(2,1)S(1)}, u32[]{:S(2)}, u32[]{:S(2)}) collective-permute-start(bf16[14,128,128]{2,1,0:T(8,128)(2,1)} %bitcast.29), channel_id=1, source_target_pairs={{0,24},{8,0},{16,8},{24,16},{1,25},{9,1},{17,9},{25,17},{2,26},{10... | collective-permute-start | bytes 1376264 | tf_op jit(solution)/shard_map/ppermute | solution.py:12
  10.4 0.5 collective-permute-start
  11.0 2.9 %broadcast_select_fusion.7 = (bf16[14,128,128]{2,1,0:T(8,128)(2,1)}, bf16[14,128,128]{2,1,0:T(8,128)(2,1)}, bf16[14,128,128]{2,1,0:T(8,128)(2,1)}, bf16[14,128,1...) fusion(pred[]{:T(512)S(6)} %eq.101, ...), kind=kLoop, calls=%fused_computation.48 | loop fusion | flops 1835008 | bytes 4128776 | tf_op jit(solution)/shard_map/jit(_where)/select_n | solution.py:16
  13.9 0.0 copy-start
  13.9 0.0 all-reduce.4.cloned.1.call-update
  13.9 0.6 copy-done
  14.5 9.4 %all-reduce = (s32[14]{0:T(128)S(1)}, s32[14]{0:T(128)S(1)}, s32[14]{0:T(128)S(1)}, s32[14]{0:T(128)S(1)}, s32[14]{0:T(128)S(1)}, /*index=5*/s32[14]{0:T(128)S(1)}, s32[14]{0:T(128)S(1)}, s32[14]{0:T(128)S(1)}) all-reduce(s32[14]{0:T(128)S(1)} %get-tuple-element.62, ...), channel_id=1, replica_groups=mesh['row'=4,'col'=8] {'col'}, use_global_device_ids=true, to_apply=%region_14.17 | all-reduce | flops 112 | bytes 896 | tf_op jit(solution)/shard_map/psum | solution.py:17
  24.2 0.7 gather_fusion.2
  24.8 0.0 copy-done.1
  24.9 0.6 gather_fusion.3
  25.5 0.7 gather_fusion
  26.2 0.6 gather_fusion.1
  26.8 0.0 collective-permute-done
  26.8 1.5 %collective-permute-start.2 = (s32[14]{0:T(128)S(1)}, s32[14]{0:T(128)S(1)}, u32[]{:S(2)}, u32[]{:S(2)}) collective-permute-start(s32[14]{0:T(128)S(1)} %collective-permute-done), channel_id=1, source_target_pairs={{0,24},{8,0},{16,8},{24,16},{1,25},{9,1},{17,9},{25,17},{2,26},{10... | collective-permute-start | bytes 176 | tf_op jit(solution)/shard_map/ppermute | solution.py:12
  28.3 0.7 gather_fusion.6
  29.0 0.7 gather_fusion.4
  29.7 0.0 collective-permute-done.1
  29.7 0.6 collective-permute-start.3
  30.2 0.2 collective-permute-done.2
  30.4 2.4 %collective-permute-start.4 = (s32[14]{0:T(128)S(1)}, s32[14]{0:T(128)S(1)}, u32[]{:S(2)}, u32[]{:S(2)}) collective-permute-start(s32[14]{0:T(128)S(1)} %collective-permute-done.2), channel_id=1, source_target_pairs={{0,24},{8,0},{16,8},{24,16},{1,25},{9,1},{17,9},{25,17},{2,26},{10... | collective-permute-start | bytes 176 | tf_op jit(solution)/shard_map/ppermute | solution.py:12
  32.8 0.7 gather_fusion.10
  33.4 0.7 gather_fusion.8
  34.1 6.3 %collective-permute-done.4 = s32[14]{0:T(128)S(1)} collective-permute-done((s32[14]{0:T(128)S(1)}, s32[14]{0:T(128)S(1)}, u32[]{:S(2)}, u32[]{:S(2)}) %collective-permute-start.4) | collective-permute-done | bytes 88 | tf_op jit(solution)/shard_map/ppermute | solution.py:12
  40.5 0.7 gather_fusion.14
  41.1 0.0 collective-permute-done.3
  41.1 1.4 %collective-permute-start.5 = (bf16[14,128,128]{2,1,0:T(8,128)(2,1)S(1)}, bf16[14,128,128]{2,1,0:T(8,128)(2,1)S(1)}, u32[]{:S(2)}, u32[]{:S(2)}) collective-permute-start(bf16[14,128,128]{2,1,0:T(8,128)(2,1)S(1)} %collective-permute-done.3), channel_id=1, source_target_pairs={{0,24},{8,0},{16,8},{24,16},{1,25},{9,1},{17,9},{25,17},{2,26},{10... | collective-permute-start | bytes 1376264 | tf_op jit(solution)/shard_map/ppermute | solution.py:12
  42.6 0.7 gather_fusion.12
  43.2 0.0 copy-done.10
  43.3 0.1 copy.19
  43.4 0.1 copy.18
  43.4 0.1 copy.17
  43.5 0.1 copy.16
  43.6 0.1 copy.15
  43.7 0.1 copy.14
  43.8 0.1 copy.13
  43.9 0.1 copy.12
  44.0 0.6 gather_fusion.7
  44.7 0.6 gather_fusion.5
  45.3 1.4 %gather_fusion.11 = bf16[14,128,128]{2,1,0:T(8,128)(2,1)} fusion(bf16[14,128,128]{2,1,0:T(8,128)(2,1)S(1)} %collective-permute-done.3, s32[1024]{0:T(1024)S(1)} %pad_clamp_fusion.2), kind=kCustom, calls=%fused_computation.13.clone | custom fusion | bytes 917560 | tf_op jit(solution)/shard_map/jit(_take)/gather | solution.py:22
  46.7 0.6 gather_fusion.9
  47.3 3.6 %collective-permute-done.5 = bf16[14,128,128]{2,1,0:T(8,128)(2,1)S(1)} collective-permute-done((bf16[14,128,128]{2,1,0:T(8,128)(2,1)S(1)}, bf16[14,128,128]{2,1,0:T(8,128)(2,1)S(1)}, u32[]{:S(2)}, u32[]{:S(2)}) %collective-permute-start.5) | collective-permute-done | bytes 458784 | tf_op jit(solution)/shard_map/ppermute | solution.py:12
  50.9 1.4 %gather_fusion.15 = bf16[14,128,128]{2,1,0:T(8,128)(2,1)} fusion(bf16[14,128,128]{2,1,0:T(8,128)(2,1)S(1)} %collective-permute-done.5, s32[1024]{0:T(1024)S(1)} %pad_clamp_fusion), kind=kCustom, calls=%fused_computation.15.clone | custom fusion | bytes 917560 | tf_op jit(solution)/shard_map/jit(_take)/gather | solution.py:22
  52.3 0.6 gather_fusion.13
  53.0 50.6 %all-reduce.4.cloned.1.call-done = (bf16[14,128,128]{2,1,0:T(8,128)(2,1)}, bf16[14,128,128]{2,1,0:T(8,128)(2,1)}, bf16[14,128,128]{2,1,0:T(8,128)(2,1)}, bf16[14...) async-done(((bf16[14,128,128]{2,1,0:T(8,128)(2,1)}, ...) | async-done | bytes 3670032 | tf_op jit(solution)/shard_map/psum | solution.py:17
  103.6 1.6 %fusion = f32[14,128,128]{2,1,0:T(8,128)S(1)} fusion(bf16[14,128,128]{2,1,0:T(8,128)(2,1)} %get-tuple-element.15, bf16[14,128,128]{2,1,0:T(8,128)(2,1)} %gather_fusion.15, pred[14]{0:T(512)(128)(4,1)S(1)} %get-tuple-element.37), kind=kOutput, calls=%fused_computation.17 | convolution fusion | flops 58949632 | bytes 1835022 | tf_op jit(solution)/shard_map/mab,mbc->mac/dot_general | solution.py:24
  105.2 0.0 copy-done.9
  105.2 0.0 copy-start.2
  105.2 0.0 copy-start.8
  105.2 0.4 fusion.2
  105.5 0.6 copy-done.2
  106.2 0.1 copy-done.8
  106.3 0.4 fusion.4
  106.7 0.7 copy-done.7
  107.3 0.4 fusion.6
  107.7 0.7 copy-done.6
  108.4 0.4 fusion.8
  108.7 0.7 copy-done.5
  109.4 0.4 fusion.10
  109.7 0.7 copy-done.4
  110.4 0.4 fusion.12
  110.8 0.7 copy-done.3
  111.4 0.4 fusion.14
  111.8 2.3 %add_convert_fusion = bf16[14,2,128,128]{3,2,1,0:T(8,128)(2,1)} fusion(f32[14,128,128]{2,1,0:T(8,128)S(1)} %fusion, f32[14,2]{1,0:T(8,128)S(1)} %copy.19, f32[14,128,128]{2,1,0:T(8,128)S(1)} %fusion.2, f32[14,2]{1,0:T(8,128)S(1)} %copy.18, f32[14,128,128]{2,1,0:T(8,128)S(1)} %fusion.4, f32[14,2]{1,0:T(8,128)S(1)} %copy.17, f32[14,128,128]{2,1,0:T(8,128)S(1)} %fusion.6, ...), kind=kLoop, calls=%fused_computation.16 | loop fusion | flops 7340032 | bytes 8258432 | tf_op jit(solution)/shard_map/convert_element_type | solution.py:60
  (34 shorter events, 0.2 us)
Async XLA Ops:
  6.5 97.0 %all-reduce.4.cloned.1.call-start = ((), (), s32[]{:S(2)}) async-start(), calls=%async_computation | async-start | bytes 7340032 | tf_op jit(solution)/shard_map/psum | solution.py:17
  6.5 23.1 %collective-permute-start.1 = (bf16[14,128,128]{2,1,0:T(8,128)(2,1)}, bf16[14,128,128]{2,1,0:T(8,128)(2,1)S(1)}, u32[]{:S(2)}, u32[]{:S(2)}) collective-permute-start(bf16[14,128,128]{2,1,0:T(8,128)(2,1)} %bitcast.29), channel_id=1, source_target_pairs={{0,24},{8,0},{16,8},{24,16},{1,25},{9,1},{17,9},{25,17},{2,26},{10... | collective-permute-start | bytes 1376264 | tf_op jit(solution)/shard_map/ppermute | solution.py:12
  10.4 16.4 %collective-permute-start = (s32[14]{0:T(128)}, s32[14]{0:T(128)S(1)}, u32[]{:S(2)}, u32[]{:S(2)}) collective-permute-start(s32[14]{0:T(128)} %bitcast.26), channel_id=1, source_target_pairs={{0,24},{8,0},{16,8},{24,16},{1,25},{9,1},{17,9},{25,17},{2,26},{10... | collective-permute-start | bytes 176 | tf_op jit(solution)/shard_map/ppermute | solution.py:12
  13.9 0.7 copy-start
  14.5 10.3 %copy-start.1 = (bf16[14,1,128,128]{3,2,1,0:T(8,128)(2,1)S(1)}, bf16[14,1,128,128]{3,2,1,0:T(8,128)(2,1)}, u32[]{:S(2)}) copy-start(bf16[14,1,128,128]{3,2,1,0:T(8,128)(2,1)} %param.7) | copy-start | bytes 1376260
  26.8 3.6 %collective-permute-start.2 = (s32[14]{0:T(128)S(1)}, s32[14]{0:T(128)S(1)}, u32[]{:S(2)}, u32[]{:S(2)}) collective-permute-start(s32[14]{0:T(128)S(1)} %collective-permute-done), channel_id=1, source_target_pairs={{0,24},{8,0},{16,8},{24,16},{1,25},{9,1},{17,9},{25,17},{2,26},{10... | collective-permute-start | bytes 176 | tf_op jit(solution)/shard_map/ppermute | solution.py:12
  29.7 11.4 %collective-permute-start.3 = (bf16[14,128,128]{2,1,0:T(8,128)(2,1)S(1)}, bf16[14,128,128]{2,1,0:T(8,128)(2,1)S(1)}, u32[]{:S(2)}, u32[]{:S(2)}) collective-permute-start(bf16[14,128,128]{2,1,0:T(8,128)(2,1)S(1)} %collective-permute-done.1), channel_id=1, source_target_pairs={{0,24},{8,0},{16,8},{24,16},{1,25},{9,1},{17,9},{25,17},{2,26},{10... | collective-permute-start | bytes 1376264 | tf_op jit(solution)/shard_map/ppermute | solution.py:12
  30.4 10.0 %collective-permute-start.4 = (s32[14]{0:T(128)S(1)}, s32[14]{0:T(128)S(1)}, u32[]{:S(2)}, u32[]{:S(2)}) collective-permute-start(s32[14]{0:T(128)S(1)} %collective-permute-done.2), channel_id=1, source_target_pairs={{0,24},{8,0},{16,8},{24,16},{1,25},{9,1},{17,9},{25,17},{2,26},{10... | collective-permute-start | bytes 176 | tf_op jit(solution)/shard_map/ppermute | solution.py:12
  33.4 9.8 %copy-start.10 = (s32[14,2]{0,1:T(2,128)S(1)}, s32[14,2]{0,1:T(2,128)}, u32[]{:S(2)}) copy-start(s32[14,2]{0,1:T(2,128)} %param.9) | copy-start | bytes 340
  41.1 9.8 %collective-permute-start.5 = (bf16[14,128,128]{2,1,0:T(8,128)(2,1)S(1)}, bf16[14,128,128]{2,1,0:T(8,128)(2,1)S(1)}, u32[]{:S(2)}, u32[]{:S(2)}) collective-permute-start(bf16[14,128,128]{2,1,0:T(8,128)(2,1)S(1)} %collective-permute-done.3), channel_id=1, source_target_pairs={{0,24},{8,0},{16,8},{24,16},{1,25},{9,1},{17,9},{25,17},{2,26},{10... | collective-permute-start | bytes 1376264 | tf_op jit(solution)/shard_map/ppermute | solution.py:12
  103.6 1.6 %copy-start.9 = (bf16[14,128,128]{2,1,0:T(8,128)(2,1)S(1)}, bf16[14,128,128]{2,1,0:T(8,128)(2,1)}, u32[]{:S(2)}) copy-start(bf16[14,128,128]{2,1,0:T(8,128)(2,1)} %get-tuple-element.16) | copy-start | bytes 1376260
  105.2 1.0 copy-start.2
  105.2 1.1 copy-start.8
  106.3 1.0 copy-start.7
  107.3 1.0 copy-start.6
  108.4 1.0 copy-start.5
  109.4 1.0 copy-start.4
  110.4 1.0 copy-start.3
Sparse Core Ops, SparseCore 0:
  14.0 89.5 all-reduce.3
where the time goes:
time: 121 us
  waiting for transfers between devices  60.8 us (50%)
  local copies, waits for them, and re-layouts  17.3 us (14%)
  between operations  13.7 us (11%)
  starting transfers between devices  10.3 us (9%)
  blocking collectives  9.43 us (8%)
  other arithmetic  5.35 us (4%)
  matrix products  4.04 us (3%)
    psum x1, waiting for transfers between devices, broadcast(): return lax.psum(kept, axis)  50.6 us
    ppermute x6, starting transfers between devices, passed_along(): return lax.ppermute(value, axis, pairs)  10.3 us
    ppermute x6, waiting for transfers between devices, passed_along(): return lax.ppermute(value, axis, pairs)  10.1 us
    psum x1, blocking collectives, broadcast(): return lax.psum(kept, axis)  9.43 us
    gather x8, local copies, waits for them, and re-layouts, add_products(): chosen = jnp.take(b_blocks, index, axis=0)  6.57 us
    gather x8, local copies, waits for them, and re-layouts, add_products(): landing = jnp.take(b_cols, index, axis=0)  5.26 us
    unnamed x22, local copies, waits for them, and re-layouts  4.7 us
    dot_general x8, matrix products, add_products(): jnp.einsum('mab,mbc->mac', a_blocks, chosen, preferred_element_type=jnp.f...  4.04 us
  transfers between devices with their start and end apart: 7, of which 4 were waited for; matrix products, arithmetic and copies ran while one was open for 13% of the time, Pallas kernels for 0%

commit v1 on v0

--- a/solution.py
+++ b/solution.py
@@ -14,7 +14,7 @@
 
 def broadcast(value, axis, source):
     kept = jnp.where(lax.axis_index(axis) == source, value, 0).astype(value.dtype)
-    return lax.psum(kept, axis)
+    return jnp.sum(lax.all_gather(kept, axis), axis=0)
 
 
 def add_products(total, a_blocks, a_cols, b_blocks, b_cols, targets, offset):

time: 121 us -> 373 us (3.08)
  waiting for transfers between devices: 60.8 us -> 286 us
  other arithmetic: 5.35 us -> 34.3 us
    all_gather x0 -> x8, waiting for transfers between devices: none -> 270 us  [broadcast(): return jnp.sum(lax.all_gather(kept, axis), axis=0)]
    psum x1 -> x0, waiting for transfers between devices: 50.6 us -> none  [broadcast(): return lax.psum(kept, axis)]
    reduce_sum x0 -> x16, other arithmetic: none -> 28.3 us  [broadcast(): return jnp.sum(lax.all_gather(kept, axis), axis=0)]
    psum x1 -> x0, blocking collectives: 9.43 us -> none  [broadcast(): return lax.psum(kept, axis)]
    unnamed x0 -> x1, blocking collectives: none -> 9.39 us
  transfers between devices with their start and end apart: 7 -> 14, of which waited for: 4 -> 10; matrix products, arithmetic and copies ran while one was open for 13% -> 11% of each run, Pallas kernels for 0% -> 0%
where the time goes in v1:
time: 373 us
  waiting for transfers between devices  286 us (77%)
  other arithmetic  34.3 us (9%)
  local copies, waits for them, and re-layouts  15.2 us (4%)
  between operations  14.5 us (4%)
  starting transfers between devices  10.8 us (3%)
  blocking collectives  9.39 us (3%)
    all_gather x8, waiting for transfers between devices, broadcast(): return jnp.sum(lax.all_gather(kept, axis), axis=0)  270 us
    reduce_sum x16, other arithmetic, broadcast(): return jnp.sum(lax.all_gather(kept, axis), axis=0)  28.3 us
    ppermute x6, waiting for transfers between devices, passed_along(): return lax.ppermute(value, axis, pairs)  11.7 us
    ppermute x6, starting transfers between devices, passed_along(): return lax.ppermute(value, axis, pairs)  10.5 us
    unnamed x1, blocking collectives  9.39 us
  transfers between devices with their start and end apart: 14, of which 10 were waited for; matrix products, arithmetic and copies ran while one was open for 11% of the time, Pallas kernels for 0%

profile of v1, /device:TPU:0, one launch (start us, length us, event | category | flops | bytes accessed | tf_op | source)
XLA Modules:
  0.0 372.9 jit_solution(15612006045439190873)
XLA Ops:
  6.5 2.9 broadcast_select_fusion.7
  9.5 0.7 all-gather.33.cloned.1.call-update
  10.3 0.7 all-gather.35.cloned.1.call-update
  11.0 0.5 all-gather.39.cloned.1.call-update
  11.6 0.5 all-gather.29.cloned.1.call-update
  12.2 0.5 all-gather.31.cloned.1.call-update
  12.7 0.7 all-gather.25.cloned.1.call-update
  13.5 3.9 %collective-permute-start.1 = (bf16[14,128,128]{2,1,0:T(8,128)(2,1)S(1)}, bf16[14,128,128]{2,1,0:T(8,128)(2,1)S(1)}, u32[]{:S(2)}, u32[]{:S(2)}) collective-permute-start(bf16[14,128,128]{2,1,0:T(8,128)(2,1)S(1)} %bitcast.70), channel_id=1, source_target_pairs={{0,24},{8,0},{16,8},{24,16},{1,25},{9,1},{17,9},{25,17},{2,26},{10... | collective-permute-start | bytes 1376264 | tf_op jit(solution)/shard_map/ppermute | solution.py:12
  17.5 0.5 collective-permute-start
  18.0 0.6 dynamic-slice
  19.2 0.1 fusion.45
  19.9 9.4 %all-reduce.8 = (s32[112]{0:T(128)S(1)}, s32[112]{0:T(128)S(1)}, s32[112]{0:T(128)S(1)}, s32[112]{0:T(128)S(1)}, s32[112]{0:T(128)S(1)}, /*index=5*/s32[112]{0:T(128)S(1)}, s32[112]{0:T(128)S(1)}, s32[112]{0:T(128)S(1)}) all-reduce(s32[112]{0:T(128)S(1)} %fusion.47, s32[112]{0:T(128)S(1)} %fusion.45, ...), channel_id=16, replica_groups=mesh['row'=4,'col'=8] {'col'}, use_global_device_ids=true, to_apply=%add.7 | all-reduce | flops 896 | bytes 7168
  30.0 0.7 gather_fusion.2
  31.0 0.6 gather_fusion.1
  31.7 0.7 gather_fusion
  32.3 0.6 gather_fusion.3
  33.0 1.5 collective-permute-start.2
  34.5 0.7 gather_fusion.4
  35.1 0.7 gather_fusion.6
  35.8 0.6 collective-permute-start.3
  36.4 0.2 collective-permute-done.2
  36.6 2.3 collective-permute-start.4
  38.9 0.7 gather_fusion.8
  39.6 0.7 gather_fusion.10
  40.3 6.7 %collective-permute-done.4 = s32[14]{0:T(128)S(1)} collective-permute-done((s32[14]{0:T(128)S(1)}, s32[14]{0:T(128)S(1)}, u32[]{:S(2)}, u32[]{:S(2)}) %collective-permute-start.4) | collective-permute-done | bytes 88 | tf_op jit(solution)/shard_map/ppermute | solution.py:12
  46.9 0.7 gather_fusion.14
  47.6 1.7 collective-permute-start.5
  49.3 0.7 gather_fusion.12
  50.0 0.1 copy.20
  50.7 0.6 gather_fusion.5
  51.4 0.6 gather_fusion.7
  52.0 1.4 gather_fusion.9
  53.4 0.6 gather_fusion.11
  54.0 4.8 %collective-permute-done.5 = bf16[14,128,128]{2,1,0:T(8,128)(2,1)S(1)} collective-permute-done((bf16[14,128,128]{2,1,0:T(8,128)(2,1)S(1)}, bf16[14,128,128]{2,1,0:T(8,128)(2,1)S(1)}, u32[]{:S(2)}, u32[]{:S(2)}) %collective-permute-start.5) | collective-permute-done | bytes 458784 | tf_op jit(solution)/shard_map/ppermute | solution.py:12
  58.9 1.4 gather_fusion.13
  60.2 0.6 gather_fusion.15
  60.9 3.8 %bitcast_reduce_fusion.1 = bf16[14,128,128]{2,1,0:T(8,128)(2,1)} fusion(bf16[8,14,128,128]{3,2,1,0:T(8,128)(2,1)} %bitcast.73), kind=kLoop, calls=%fused_computation.17 | loop fusion | flops 1605632 | bytes 4128768 | tf_op jit(solution)/shard_map/reduce_sum | solution.py:17
  64.7 33.5 %all-gather.33.cloned.1.call-done = bf16[112,1,128,128]{3,2,1,0:T(8,128)(2,1)} async-done(((bf16[14,1,128,128]{3,2,1,0:T(8,128)(2,1)}), bf16[112,1,128,128]{3,2,1,0:T(8,128)(2,1)}) %all-gather.33.cloned.1.call-update) | async-done | bytes 3670032 | tf_op jit(solution)/shard_map/all_gather | solution.py:17
  98.2 3.6 bitcast_reduce_fusion.3
  101.8 39.6 %all-gather.35.cloned.1.call-done = bf16[112,1,128,128]{3,2,1,0:T(8,128)(2,1)} async-done(((bf16[14,1,128,128]{3,2,1,0:T(8,128)(2,1)}), bf16[112,1,128,128]{3,2,1,0:T(8,128)(2,1)}) %all-gather.35.cloned.1.call-update) | async-done | bytes 3670032 | tf_op jit(solution)/shard_map/all_gather | solution.py:17
  141.4 3.6 bitcast_reduce_fusion.2
  145.0 39.4 %all-gather.39.cloned.1.call-done = bf16[112,1,128,128]{3,2,1,0:T(8,128)(2,1)} async-done(((bf16[14,1,128,128]{3,2,1,0:T(8,128)(2,1)}), bf16[112,1,128,128]{3,2,1,0:T(8,128)(2,1)}) %all-gather.39.cloned.1.call-update) | async-done | bytes 3670032 | tf_op jit(solution)/shard_map/all_gather | solution.py:17
  184.4 3.6 bitcast_reduce_fusion
  188.0 39.4 %all-gather.29.cloned.1.call-done = bf16[112,1,128,128]{3,2,1,0:T(8,128)(2,1)} async-done(((bf16[14,1,128,128]{3,2,1,0:T(8,128)(2,1)}), bf16[112,1,128,128]{3,2,1,0:T(8,128)(2,1)}) %all-gather.29.cloned.1.call-update) | async-done | bytes 3670032 | tf_op jit(solution)/shard_map/all_gather | solution.py:17
  227.3 3.6 bitcast_reduce_fusion.5
  230.9 39.4 %all-gather.31.cloned.1.call-done = bf16[112,1,128,128]{3,2,1,0:T(8,128)(2,1)} async-done(((bf16[14,1,128,128]{3,2,1,0:T(8,128)(2,1)}), bf16[112,1,128,128]{3,2,1,0:T(8,128)(2,1)}) %all-gather.31.cloned.1.call-update) | async-done | bytes 3670032 | tf_op jit(solution)/shard_map/all_gather | solution.py:17
  270.3 3.6 bitcast_reduce_fusion.4
  274.0 39.5 %all-gather.25.cloned.1.call-done = bf16[112,1,128,128]{3,2,1,0:T(8,128)(2,1)} async-done(((bf16[14,1,128,128]{3,2,1,0:T(8,128)(2,1)}), bf16[112,1,128,128]{3,2,1,0:T(8,128)(2,1)}) %all-gather.25.cloned.1.call-update) | async-done | bytes 3670032 | tf_op jit(solution)/shard_map/all_gather | solution.py:17
  313.5 3.6 bitcast_reduce_fusion.7
  317.1 39.6 %all-gather.27.cloned.1.call-done = bf16[112,1,128,128]{3,2,1,0:T(8,128)(2,1)} async-done(((bf16[14,1,128,128]{3,2,1,0:T(8,128)(2,1)}), bf16[112,1,128,128]{3,2,1,0:T(8,128)(2,1)}) %all-gather.27.cloned.1.call-update) | async-done | bytes 3670032 | tf_op jit(solution)/shard_map/all_gather | solution.py:17
  356.6 2.7 bitcast_reduce_fusion.6
  359.4 0.4 fusion.2
  359.8 0.6 copy-done.2
  360.4 0.1 copy-done.5
  360.5 0.4 fusion.6
  360.9 0.4 fusion.4
  361.3 0.3 copy-done.7
  361.6 0.4 fusion
  362.0 0.4 fusion.10
  362.3 0.3 copy-done.9
  362.6 0.4 fusion.8
  363.0 0.4 fusion.14
  363.4 0.4 fusion.12
  363.7 2.3 add_convert_fusion
  (99 shorter events, 2.6 us)
Async XLA Ops:
  6.5 54.4 %all-gather.37.cloned.1.call-start = ((), (), s32[]{:S(2)}) async-start(), calls=%async_computation.6 | async-start | bytes 4128768 | tf_op jit(solution)/shard_map/all_gather | solution.py:17
  9.4 4.1 %copy-start.1 = (bf16[14,1,128,128]{3,2,1,0:T(8,128)(2,1)S(1)}, bf16[14,1,128,128]{3,2,1,0:T(8,128)(2,1)}, u32[]{:S(2)}) copy-start(bf16[14,1,128,128]{3,2,1,0:T(8,128)(2,1)} %param.7) | copy-start | bytes 1376260
  9.4 8.0 %copy-start = (s32[14,1]{0,1:T(1,128)S(1)}, s32[14,1]{0,1:T(1,128)}, u32[]{:S(2)}) copy-start(s32[14,1]{0,1:T(1,128)} %param.8) | copy-start | bytes 172
  9.4 8.6 %copy-start.12 = (u32[32]{0:T(128)S(1)}, u32[32]{0:T(128)}, u32[]{:S(2)}) copy-start(u32[32]{0:T(128)} %constant.77) | copy-start | bytes 388
  9.5 88.7 %all-gather.33.cloned.1.call-start = ((), (), s32[]{:S(2)}) async-start(), calls=%async_computation.4 | async-start | bytes 4128768 | tf_op jit(solution)/shard_map/all_gather | solution.py:17
  10.2 131.1 %all-gather.35.cloned.1.call-start = ((), (), s32[]{:S(2)}) async-start(), calls=%async_computation.5 | async-start | bytes 4128768 | tf_op jit(solution)/shard_map/all_gather | solution.py:17
  11.0 173.4 %all-gather.39.cloned.1.call-start = ((), (), s32[]{:S(2)}) async-start(), calls=%async_computation.7 | async-start | bytes 4128768 | tf_op jit(solution)/shard_map/all_gather | solution.py:17
  11.5 215.8 %all-gather.29.cloned.1.call-start = ((), (), s32[]{:S(2)}) async-start(), calls=%async_computation.2 | async-start | bytes 4128768 | tf_op jit(solution)/shard_map/all_gather | solution.py:17
  12.1 258.2 %all-gather.31.cloned.1.call-start = ((), (), s32[]{:S(2)}) async-start(), calls=%async_computation.3 | async-start | bytes 4128768 | tf_op jit(solution)/shard_map/all_gather | solution.py:17
  12.7 300.8 %all-gather.25.cloned.1.call-start = ((), (), s32[]{:S(2)}) async-start(), calls=%async_computation | async-start | bytes 4128768 | tf_op jit(solution)/shard_map/all_gather | solution.py:17
  13.4 343.2 %all-gather.27.cloned.1.call-start = ((), (), s32[]{:S(2)}) async-start(), calls=%async_computation.1 | async-start | bytes 4128768 | tf_op jit(solution)/shard_map/all_gather | solution.py:17
  13.5 22.3 %collective-permute-start.1 = (bf16[14,128,128]{2,1,0:T(8,128)(2,1)S(1)}, bf16[14,128,128]{2,1,0:T(8,128)(2,1)S(1)}, u32[]{:S(2)}, u32[]{:S(2)}) collective-permute-start(bf16[14,128,128]{2,1,0:T(8,128)(2,1)S(1)} %bitcast.70), channel_id=1, source_target_pairs={{0,24},{8,0},{16,8},{24,16},{1,25},{9,1},{17,9},{25,17},{2,26},{10... | collective-permute-start | bytes 1376264 | tf_op jit(solution)/shard_map/ppermute | solution.py:12
  17.5 15.5 %collective-permute-start = (s32[14]{0:T(128)S(1)}, s32[14]{0:T(128)S(1)}, u32[]{:S(2)}, u32[]{:S(2)}) collective-permute-start(s32[14]{0:T(128)S(1)} %bitcast.67), channel_id=1, source_target_pairs={{0,24},{8,0},{16,8},{24,16},{1,25},{9,1},{17,9},{25,17},{2,26},{10... | collective-permute-start | bytes 176 | tf_op jit(solution)/shard_map/ppermute | solution.py:12
  32.3 17.6 %copy-start.11 = (s32[14,2]{0,1:T(2,128)S(1)}, s32[14,2]{0,1:T(2,128)}, u32[]{:S(2)}) copy-start(s32[14,2]{0,1:T(2,128)} %param.9) | copy-start | bytes 340
  33.0 3.6 collective-permute-start.2
  35.8 11.8 %collective-permute-start.3 = (bf16[14,128,128]{2,1,0:T(8,128)(2,1)S(1)}, bf16[14,128,128]{2,1,0:T(8,128)(2,1)S(1)}, u32[]{:S(2)}, u32[]{:S(2)}) collective-permute-start(bf16[14,128,128]{2,1,0:T(8,128)(2,1)S(1)} %collective-permute-done.1), channel_id=1, source_target_pairs={{0,24},{8,0},{16,8},{24,16},{1,25},{9,1},{17,9},{25,17},{2,26},{10... | collective-permute-start | bytes 1376264 | tf_op jit(solution)/shard_map/ppermute | solution.py:12
  36.6 10.3 %collective-permute-start.4 = (s32[14]{0:T(128)S(1)}, s32[14]{0:T(128)S(1)}, u32[]{:S(2)}, u32[]{:S(2)}) collective-permute-start(s32[14]{0:T(128)S(1)} %collective-permute-done.2), channel_id=1, source_target_pairs={{0,24},{8,0},{16,8},{24,16},{1,25},{9,1},{17,9},{25,17},{2,26},{10... | collective-permute-start | bytes 176 | tf_op jit(solution)/shard_map/ppermute | solution.py:12
  47.6 11.3 %collective-permute-start.5 = (bf16[14,128,128]{2,1,0:T(8,128)(2,1)S(1)}, bf16[14,128,128]{2,1,0:T(8,128)(2,1)S(1)}, u32[]{:S(2)}, u32[]{:S(2)}) collective-permute-start(bf16[14,128,128]{2,1,0:T(8,128)(2,1)S(1)} %collective-permute-done.3), channel_id=1, source_target_pairs={{0,24},{8,0},{16,8},{24,16},{1,25},{9,1},{17,9},{25,17},{2,26},{10... | collective-permute-start | bytes 1376264 | tf_op jit(solution)/shard_map/ppermute | solution.py:12
  356.6 2.8 copy-start.3
  356.6 2.8 copy-start.4
  359.4 1.0 copy-start.2
  359.4 1.1 copy-start.5
  359.4 1.5 copy-start.6
  360.5 1.1 copy-start.7
  360.9 1.1 copy-start.8
  361.6 1.1 copy-start.9
  362.0 1.1 copy-start.10
Sparse Core Ops, SparseCore 0:
  9.6 45.4 all-gather.36
  56.7 41.4 all-gather.32
  99.9 41.4 all-gather.34
  142.9 41.4 all-gather.38
  185.8 41.4 all-gather.28
  228.8 41.4 all-gather.30
  272.0 41.4 all-gather.24
  315.1 41.4 all-gather.26
